TPU v7x, 256 devices: a whole 4x4x8 slice. The times are simulated.
256 devices in a mesh: pix: 16 (over y, x_hi, core), tm: 16 (over x_lo, z).
Axes of the slice: x: 4 (x_hi: 2, x_lo: 2; x = x_hi * 2 + x_lo), y: 4, z: 8, core: 2. Of those that a mesh axis runs over, the one named last changes fastest.
Arguments:
- raw_movie: float32 [128, 256, 8192], P('pix', None, 'tm'), may hold values from 0.05 to 2
- footprints: float32 [256, 32768], P('tm', 'pix'), may hold values from 0.05 to 1
- traces: float32 [256, 8192], P('pix', 'tm'), may hold values from 0.05 to 1
Outputs:
- denoised: float32 [128, 256, 8192], P('pix', None, 'tm')
- new_footprints: float32 [256, 32768], P('tm', 'pix')
- new_traces: float32 [256, 8192], P('pix', 'tm')
All inputs are finite; a program needn't handle non-finite values.
Results may differ from a plain program's by a relative error of at most 0.00013.
Values sent between devices are 32-bit elements; how exact they have to be, the bound alone decides.
A program may use at most 64 MiB of HBM per device.

v0:
```python
import jax
import jax.numpy as jnp
from jax import lax
from jax.sharding import PartitionSpec as P

edge_scale = 0.5
step_size = 0.24


def with_halo(cells, sides, width):
    for axis, dim in sides:
        count = lax.axis_size(axis)
        ends = count - 1
        head = lax.slice_in_dim(cells, 0, width, axis=dim)
        tail = lax.slice_in_dim(cells, cells.shape[dim] - width, cells.shape[dim], axis=dim)
        cells = jnp.concatenate(
            [
                lax.ppermute(tail, axis, [(i, (i + 1) % count) for i in range(ends)]),
                cells,
                lax.ppermute(head, axis, [((i + 1) % count, i) for i in range(ends)]),
            ],
            axis=dim,
        )
    return cells


def flux_term(change):
    return change / (1.0 + change / edge_scale * (change / edge_scale))


def substep(extended):
    middle = extended[1:-1]
    padded = jnp.pad(middle, ((0, 0), (1, 1), (0, 0)))
    summed = flux_term(extended[:-2] - middle) + flux_term(extended[2:] - middle)
    summed = summed + flux_term(padded[:, :-2] - middle) + flux_term(padded[:, 2:] - middle)
    return middle + step_size * summed


def matmul_hi(left, right):
    return jnp.dot(left, right, precision=lax.Precision.HIGHEST, preferred_element_type=jnp.float32)


def contract_last(left, right):
    return lax.dot_general(
        left,
        right,
        (((1,), (1,)), ((), ())),
        precision=lax.Precision.HIGHEST,
        preferred_element_type=jnp.float32,
    )


def body(raw_movie, footprints, traces):
    row_count = raw_movie.shape[0]
    col_count = raw_movie.shape[1]
    frame_count = raw_movie.shape[2]
    current = raw_movie
    for repeat in range(4):
        extended = with_halo(current, (("pix", 0),), 1)
        current = substep(extended)
    pixels = current.reshape(row_count * col_count, frame_count)
    foot_full = lax.all_gather(footprints, "tm", axis=0, tiled=True)
    trace_full = lax.all_gather(traces, "pix", axis=0, tiled=True)
    rank_block = traces.shape[0]
    rank_start = lax.axis_index("pix") * rank_block
    part = foot_full
    numerator = lax.psum_scatter(matmul_hi(part, pixels), "pix", scatter_dimension=0, tiled=True)
    gram = lax.psum(contract_last(foot_full, foot_full), "pix")
    gram_rows = lax.dynamic_slice_in_dim(gram, rank_start, rank_block, 0)
    new_traces = traces * numerator / matmul_hi(gram_rows, trace_full)
    new_full = lax.all_gather(new_traces, "pix", axis=0, tiled=True)
    foot_block = footprints.shape[0]
    foot_start = lax.axis_index("tm") * foot_block
    part = new_full
    foot_numerator = lax.psum_scatter(
        contract_last(part, pixels), "tm", scatter_dimension=0, tiled=True
    )
    trace_gram = lax.psum(contract_last(new_full, new_full), "tm")
    trace_rows = lax.dynamic_slice_in_dim(trace_gram, foot_start, foot_block, 0)
    new_footprints = footprints * foot_numerator / matmul_hi(trace_rows, foot_full)
    return (current, new_footprints, new_traces)


def solution(mesh):
    placed = (P("pix", None, "tm"), P("tm", "pix"), P("pix", "tm"))
    return jax.shard_map(
        body,
        mesh=mesh,
        in_specs=placed,
        out_specs=(P("pix", None, "tm"), P("tm", "pix"), P("pix", "tm")),
        check_vma=False,
    )
```

profile of v0, /device:TPU:8, one launch (start us, length us, event | category | flops | bytes accessed | tf_op | source)
XLA Modules:
  0.0 603.0 jit_solution(13072026490475913355)
XLA Ops:
  8.5 1.9 collective-permute-start
  10.4 6.0 %collective-permute-start.1 = (f32[1,256,512]{2,1,0:T(8,128)S(1)}, f32[1,256,512]{2,1,0:T(8,128)S(1)}, u32[]{:S(2)}, u32[]{:S(2)}) collective-permute-start(f32[1,256,512]{2,1,0:T(8,128)S(1)} %get-tuple-element.13), channel_id=1, source_target_pairs={{16,0},{32,16},{48,32},{64,48},{80,64},{96,80},{112,96},{128,112},... | collective-permute-start | bytes 1572872 | tf_op jit(solution)/shard_map/ppermute | solution.py:20
  16.5 6.2 %collective-permute-done = f32[1,256,512]{2,1,0:T(8,128)S(1)} collective-permute-done((f32[1,256,512]{2,1,0:T(8,128)S(1)}, f32[1,256,512]{2,1,0:T(8,128)S(1)}, u32[]{:S(2)}, u32[]{:S(2)}) %collective-permute-start) | collective-permute-done | bytes 524320 | tf_op jit(solution)/shard_map/ppermute | solution.py:18
  22.7 2.4 collective-permute-done.1
  25.1 9.9 %multiply_add_fusion.3 = f32[8,256,512]{2,1,0:T(8,128)S(1)} fusion(f32[8,256,512]{2,1,0:T(8,128)} %param.3, f32[1,256,512]{2,1,0:T(8,128)S(1)} %collective-permute-done.1, f32[1,256,512]{2,1,0:T(8,128)S(1)} %collective-permute-done), kind=kLoop, calls=%fused_computation.19 | loop fusion | flops 28311552 | bytes 9437184 | tf_op jit(solution)/shard_map/add | solution.py:36
  35.1 3.7 collective-permute-start.2
  38.8 4.4 collective-permute-start.3
  43.3 7.8 %collective-permute-done.2 = f32[1,256,512]{2,1,0:T(8,128)S(1)} collective-permute-done((f32[1,256,512]{2,1,0:T(8,128)S(1)}, f32[1,256,512]{2,1,0:T(8,128)S(1)}, u32[]{:S(2)}, u32[]{:S(2)}) %collective-permute-start.2) | collective-permute-done | bytes 524320 | tf_op jit(solution)/shard_map/ppermute | solution.py:18
  51.0 4.5 multiply_add_fusion.2
  55.6 2.0 copy-done.1
  57.7 4.6 collective-permute-start.4
  62.3 3.3 collective-permute-start.5
  65.7 6.6 %collective-permute-done.4 = f32[1,256,512]{2,1,0:T(8,128)S(1)} collective-permute-done((f32[1,256,512]{2,1,0:T(8,128)S(1)}, f32[1,256,512]{2,1,0:T(8,128)S(1)}, u32[]{:S(2)}, u32[]{:S(2)}) %collective-permute-start.4) | collective-permute-done | bytes 524320 | tf_op jit(solution)/shard_map/ppermute | solution.py:18
  72.3 1.6 collective-permute-done.5
  73.9 9.9 %multiply_add_fusion.1 = f32[8,256,512]{2,1,0:T(8,128)S(1)} fusion(f32[8,256,512]{2,1,0:T(8,128)} %copy-done.1, f32[1,256,512]{2,1,0:T(8,128)S(1)} %collective-permute-done.5, f32[1,256,512]{2,1,0:T(8,128)S(1)} %collective-permute-done.4), kind=kLoop, calls=%fused_computation.17 | loop fusion | flops 28311552 | bytes 9437184 | tf_op jit(solution)/shard_map/add | solution.py:36
  83.9 4.1 collective-permute-start.6
  88.0 4.0 collective-permute-start.7
  92.0 15.4 %collective-permute-done.6 = f32[1,256,512]{2,1,0:T(8,128)S(1)} collective-permute-done((f32[1,256,512]{2,1,0:T(8,128)S(1)}, f32[1,256,512]{2,1,0:T(8,128)S(1)}, u32[]{:S(2)}, u32[]{:S(2)}) %collective-permute-start.6) | collective-permute-done | bytes 524320 | tf_op jit(solution)/shard_map/ppermute | solution.py:18
  107.5 5.5 multiply_add_fusion
  113.0 25.6 %all-gather.2.cloned.1.call-done = f32[256,2048]{1,0:T(8,128)} async-done(((f32[16,2048]{1,0:T(8,128)}), f32[256,2048]{1,0:T(8,128)}) %all-gather.2.cloned.1.call-update) | async-done | bytes 2097168 | tf_op jit(solution)/shard_map/all_gather | solution.py:62
  138.6 4.9 fusion.17
  143.8 8.6 %convolution_bitcast_fusion = f32[256,512]{0,1:T(8,128)S(1)} fusion(f32[2048,512]{1,0:T(8,128)} %bitcast.14, f32[256,2048]{1,0:T(8,128)S(1)} %copy-done), kind=kOutput, calls=%fused_computation.20 | convolution fusion | flops 3221225472 | bytes 6815744 | tf_op jit(solution)/shard_map/dot_general | solution.py:40
  153.4 24.2 %all_gather.10 = f32[256,512]{1,0:T(8,128)S(1)} all-gather(f32[16,512]{1,0:T(8,128)S(1)} %copy-done.3), channel_id=1, replica_groups=mesh['pix'=16,'tm'=16] {'pix'}, dimensions={0}, use_global_device_ids=true | all-gather | bytes 557056 | tf_op jit(solution)/shard_map/all_gather | solution.py:63
  177.6 99.5 %all-reduce.7.cloned.1.call-done = f32[256,256]{1,0:T(8,128)} async-done(((f32[256,256]{1,0:T(8,128)}), f32[256,256]{1,0:T(8,128)}) %all-reduce.7.cloned.1.call-update) | async-done | bytes 262160 | tf_op jit(solution)/shard_map/psum | solution.py:68
  277.1 85.2 %reduce-scatter.7.cloned.1.call-done = f32[16,512]{1,0:T(8,128)} async-done(((f32[256,512]{1,0:T(8,128)}), f32[16,512]{1,0:T(8,128)}) %reduce-scatter.7.cloned.1.call-update) | async-done | bytes 32784 | tf_op jit(solution)/shard_map/reduce_scatter | solution.py:67
  363.5 21.5 %all_gather.11 = f32[256,512]{1,0:T(8,128)S(1)} all-gather(f32[16,512]{1,0:T(8,128)S(1)} %convolution_divide_fusion), channel_id=1, replica_groups=mesh['pix'=16,'tm'=16] {'pix'}, dimensions={0}, use_global_device_ids=true | all-gather | bytes 557056 | tf_op jit(solution)/shard_map/all_gather | solution.py:71
  385.0 1.3 fusion.19
  386.4 7.2 %fusion.18 = f32[256,2048]{1,0:T(8,128)} fusion(f32[256,512]{1,0:T(8,128)S(1)} %all_gather.11, f32[2048,512]{1,0:T(8,128)} %bitcast.15), kind=kOutput, calls=%fused_computation.33 | convolution fusion | flops 3221225472 | bytes 6815744 | tf_op jit(solution)/shard_map/dot_general | solution.py:44
  393.6 127.1 %all-reduce.9.cloned.1.call-done = f32[256,256]{1,0:T(8,128)} async-done(((f32[256,256]{1,0:T(8,128)}), f32[256,256]{1,0:T(8,128)}) %all-reduce.9.cloned.1.call-update) | async-done | bytes 262160 | tf_op jit(solution)/shard_map/psum | solution.py:78
  520.7 1.8 fusion.8
  522.5 72.4 %reduce-scatter.5.cloned.1.call-done = f32[16,2048]{1,0:T(8,128)} async-done(((f32[256,2048]{1,0:T(8,128)}), f32[16,2048]{1,0:T(8,128)}) %reduce-scatter.5.cloned.1.call-update) | async-done | bytes 131088 | tf_op jit(solution)/shard_map/reduce_scatter | solution.py:75
  594.9 1.6 multiply_divide_fusion
  (27 shorter events, 4.1 us)
Async XLA Ops:
  7.2 131.4 %all-gather.2.cloned.1.call-start = ((), (), s32[]{:S(2)}) async-start(), calls=%async_computation.2 | async-start | bytes 2228224 | tf_op jit(solution)/shard_map/all_gather | solution.py:62
  8.5 14.2 %collective-permute-start = (f32[1,256,512]{2,1,0:T(8,128)S(1)}, f32[1,256,512]{2,1,0:T(8,128)S(1)}, u32[]{:S(2)}, u32[]{:S(2)}) collective-permute-start(f32[1,256,512]{2,1,0:T(8,128)S(1)} %get-tuple-element.12), channel_id=1, source_target_pairs={{0,16},{16,32},{32,48},{48,64},{64,80},{80,96},{96,112},{112,128},... | collective-permute-start | bytes 1572872 | tf_op jit(solution)/shard_map/ppermute | solution.py:18
  10.4 14.7 %collective-permute-start.1 = (f32[1,256,512]{2,1,0:T(8,128)S(1)}, f32[1,256,512]{2,1,0:T(8,128)S(1)}, u32[]{:S(2)}, u32[]{:S(2)}) collective-permute-start(f32[1,256,512]{2,1,0:T(8,128)S(1)} %get-tuple-element.13), channel_id=1, source_target_pairs={{16,0},{32,16},{48,32},{64,48},{80,64},{96,80},{112,96},{128,112},... | collective-permute-start | bytes 1572872 | tf_op jit(solution)/shard_map/ppermute | solution.py:20
  35.1 15.9 %collective-permute-start.2 = (f32[1,256,512]{2,1,0:T(8,128)S(1)}, f32[1,256,512]{2,1,0:T(8,128)S(1)}, u32[]{:S(2)}, u32[]{:S(2)}) collective-permute-start(f32[1,256,512]{2,1,0:T(8,128)S(1)} %get-tuple-element.10), channel_id=1, source_target_pairs={{0,16},{16,32},{32,48},{48,64},{64,80},{80,96},{96,112},{112,128},... | collective-permute-start | bytes 1572872 | tf_op jit(solution)/shard_map/ppermute | solution.py:18
  38.8 12.2 %collective-permute-start.3 = (f32[1,256,512]{2,1,0:T(8,128)S(1)}, f32[1,256,512]{2,1,0:T(8,128)S(1)}, u32[]{:S(2)}, u32[]{:S(2)}) collective-permute-start(f32[1,256,512]{2,1,0:T(8,128)S(1)} %get-tuple-element.11), channel_id=1, source_target_pairs={{16,0},{32,16},{48,32},{64,48},{80,64},{96,80},{112,96},{128,112},... | collective-permute-start | bytes 1572872 | tf_op jit(solution)/shard_map/ppermute | solution.py:20
  55.6 2.0 copy-start.1
  57.7 14.6 %collective-permute-start.4 = (f32[1,256,512]{2,1,0:T(8,128)S(1)}, f32[1,256,512]{2,1,0:T(8,128)S(1)}, u32[]{:S(2)}, u32[]{:S(2)}) collective-permute-start(f32[1,256,512]{2,1,0:T(8,128)S(1)} %get-tuple-element.8), channel_id=1, source_target_pairs={{0,16},{16,32},{32,48},{48,64},{64,80},{80,96},{96,112},{112,128},... | collective-permute-start | bytes 1572872 | tf_op jit(solution)/shard_map/ppermute | solution.py:18
  62.3 11.6 %collective-permute-start.5 = (f32[1,256,512]{2,1,0:T(8,128)S(1)}, f32[1,256,512]{2,1,0:T(8,128)S(1)}, u32[]{:S(2)}, u32[]{:S(2)}) collective-permute-start(f32[1,256,512]{2,1,0:T(8,128)S(1)} %get-tuple-element.9), channel_id=1, source_target_pairs={{16,0},{32,16},{48,32},{64,48},{80,64},{96,80},{112,96},{128,112},... | collective-permute-start | bytes 1572872 | tf_op jit(solution)/shard_map/ppermute | solution.py:20
  65.7 211.4 %all-reduce.7.cloned.1.call-start = ((), (), s32[]{:S(2)}) async-start(), calls=%async_computation.3 | async-start | bytes 524288 | tf_op jit(solution)/shard_map/psum | solution.py:68
  83.9 23.6 %collective-permute-start.6 = (f32[1,256,512]{2,1,0:T(8,128)S(1)}, f32[1,256,512]{2,1,0:T(8,128)S(1)}, u32[]{:S(2)}, u32[]{:S(2)}) collective-permute-start(f32[1,256,512]{2,1,0:T(8,128)S(1)} %get-tuple-element.6), channel_id=1, source_target_pairs={{0,16},{16,32},{32,48},{48,64},{64,80},{80,96},{96,112},{112,128},... | collective-permute-start | bytes 1572872 | tf_op jit(solution)/shard_map/ppermute | solution.py:18
  88.0 19.5 %collective-permute-start.7 = (f32[1,256,512]{2,1,0:T(8,128)S(1)}, f32[1,256,512]{2,1,0:T(8,128)S(1)}, u32[]{:S(2)}, u32[]{:S(2)}) collective-permute-start(f32[1,256,512]{2,1,0:T(8,128)S(1)} %get-tuple-element.7), channel_id=1, source_target_pairs={{16,0},{32,16},{48,32},{64,48},{80,64},{96,80},{112,96},{128,112},... | collective-permute-start | bytes 1572872 | tf_op jit(solution)/shard_map/ppermute | solution.py:20
  138.6 5.2 copy-start
  143.5 218.8 %reduce-scatter.7.cloned.1.call-start = ((), (), s32[]{:S(2)}) async-start(), calls=%async_computation.6 | async-start | bytes 557056 | tf_op jit(solution)/shard_map/reduce_scatter | solution.py:67
  143.8 9.7 %copy-start.3 = (f32[16,512]{1,0:T(8,128)S(1)}, f32[16,512]{1,0:T(8,128)}, u32[]{:S(2)}) copy-start(f32[16,512]{1,0:T(8,128)} %param.5) | copy-start | bytes 98308
  153.4 367.3 %all-reduce.9.cloned.1.call-start = ((), (), s32[]{:S(2)}) async-start(), calls=%async_computation.5 | async-start | bytes 524288 | tf_op jit(solution)/shard_map/psum | solution.py:78
  363.5 30.1 %copy-start.4 = (f32[16,512]{1,0:T(8,128)}, f32[16,512]{1,0:T(8,128)S(1)}, u32[]{:S(2)}) copy-start(f32[16,512]{1,0:T(8,128)S(1)} %convolution_divide_fusion) | copy-start | bytes 98308
  386.3 208.6 %copy-start.2 = (f32[16,2048]{1,0:T(8,128)S(1)}, f32[16,2048]{1,0:T(8,128)}, u32[]{:S(2)}) copy-start(f32[16,2048]{1,0:T(8,128)} %param.4) | copy-start | bytes 393220
  386.3 208.6 %reduce-scatter.5.cloned.1.call-start = ((), (), s32[]{:S(2)}) async-start(), calls=%async_computation.4 | async-start | bytes 2228224 | tf_op jit(solution)/shard_map/reduce_scatter | solution.py:75
Sparse Core Ops, SparseCore 0:
  65.8 72.7 all-gather.1
  143.7 133.4 all-reduce.6
  281.7 80.6 reduce-scatter.6
  386.5 134.1 all-reduce.8
  523.2 71.6 reduce-scatter.4
where the time goes:
time: 604 us; the launch traced here: 603 us
  waiting for transfers between devices  450 us (75%)
  blocking collectives  45.7 us (8%)
  starting transfers between devices  32.6 us (5%)
  other arithmetic  31.4 us (5%)
  matrix products  24.9 us (4%)
  between operations  14 us (2%)
    psum x1, waiting for transfers between devices, body(): trace_gram = lax.psum(contract_last(new_full, new_full), 'tm')  127 us
    psum x1, waiting for transfers between devices, body(): gram = lax.psum(contract_last(foot_full, foot_full), 'pix')  99.5 us
    reduce_scatter x1, waiting for transfers between devices, body(): lax.psum_scatter(matmul_hi(part, pixels), 'pix', scatter_dimension=0, til...  85.2 us
    reduce_scatter x1, waiting for transfers between devices, body(): lax.psum_scatter(contract_last(part, pixels), 'tm', scatter_dimension=0,...  72.4 us
    ppermute x4, waiting for transfers between devices, with_halo(): lax.ppermute(tail, axis, [(i, (i + 1) % count) for i in range(ends)])  36 us
    add x4, other arithmetic, substep(): return middle + step_size * summed  29.8 us
    all_gather x1, waiting for transfers between devices, body(): foot_full = lax.all_gather(footprints, 'tm', axis=0, tiled=True)  25.6 us
    all_gather x1, blocking collectives, body(): trace_full = lax.all_gather(traces, 'pix', axis=0, tiled=True)  24.2 us
  transfers between devices with their start and end apart: 13, of which 11 were waited for; matrix products, arithmetic and copies ran while one was open for 6% of the time, Pallas kernels for 0%

commit v1 on v0

--- a/solution.py
+++ b/solution.py
@@ -75,7 +75,7 @@
     foot_numerator = lax.psum_scatter(
         contract_last(part, pixels), "tm", scatter_dimension=0, tiled=True
     )
-    trace_gram = lax.psum(contract_last(new_full, new_full), "tm")
+    trace_gram = jnp.sum(lax.all_gather(contract_last(new_full, new_full), "tm"), axis=0)
     trace_rows = lax.dynamic_slice_in_dim(trace_gram, foot_start, foot_block, 0)
     new_footprints = footprints * foot_numerator / matmul_hi(trace_rows, foot_full)
     return (current, new_footprints, new_traces)

time: 604 us -> 546 us (0.904)
  waiting for transfers between devices: 450 us -> 391 us
    psum x1 -> x0, waiting for transfers between devices: 127 us -> none  [body(): trace_gram = lax.psum(contract_last(new_full, new_full), 'tm')]
    all_gather x0 -> x1, waiting for transfers between devices: none -> 69.6 us  [body(): lax.all_gather(contract_last(new_full, new_full), 'tm')]
  transfers between devices with their start and end apart: 13 -> 13, of which waited for: 11 -> 11; matrix products, arithmetic and copies ran while one was open for 6% -> 7% of each run, Pallas kernels for 0% -> 0%
where the time goes in v1:
time: 546 us; the launch traced here: 545 us
  waiting for transfers between devices  391 us (72%)
  blocking collectives  45.6 us (8%)
  other arithmetic  33.9 us (6%)
  starting transfers between devices  32.6 us (6%)
  matrix products  24.2 us (4%)
  between operations  14 us (3%)
    psum x1, waiting for transfers between devices, body(): gram = lax.psum(contract_last(foot_full, foot_full), 'pix')  99.7 us
    reduce_scatter x1, waiting for transfers between devices, body(): lax.psum_scatter(matmul_hi(part, pixels), 'pix', scatter_dimension=0, til...  85.2 us
    reduce_scatter x1, waiting for transfers between devices, body(): lax.psum_scatter(contract_last(part, pixels), 'tm', scatter_dimension=0,...  70.6 us
    all_gather x1, waiting for transfers between devices, body(): lax.all_gather(contract_last(new_full, new_full), 'tm')  69.6 us
    ppermute x4, waiting for transfers between devices, with_halo(): lax.ppermute(tail, axis, [(i, (i + 1) % count) for i in range(ends)])  36.1 us
    add x4, other arithmetic, substep(): return middle + step_size * summed  29.9 us
    all_gather x1, waiting for transfers between devices, body(): foot_full = lax.all_gather(footprints, 'tm', axis=0, tiled=True)  25.4 us
    all_gather x1, blocking collectives, body(): trace_full = lax.all_gather(traces, 'pix', axis=0, tiled=True)  24.2 us
  transfers between devices with their start and end apart: 13, of which 11 were waited for; matrix products, arithmetic and copies ran while one was open for 7% of the time, Pallas kernels for 0%

profile of v1, /device:TPU:8, one launch (start us, length us, event | category | flops | bytes accessed | tf_op | source)
XLA Modules:
  0.0 545.5 jit_solution(16281174521953557911)
XLA Ops:
  8.5 1.9 collective-permute-start
  10.4 6.0 %collective-permute-start.1 = (f32[1,256,512]{2,1,0:T(8,128)S(1)}, f32[1,256,512]{2,1,0:T(8,128)S(1)}, u32[]{:S(2)}, u32[]{:S(2)}) collective-permute-start(f32[1,256,512]{2,1,0:T(8,128)S(1)} %get-tuple-element.13), channel_id=1, source_target_pairs={{16,0},{32,16},{48,32},{64,48},{80,64},{96,80},{112,96},{128,112},... | collective-permute-start | bytes 1572872 | tf_op jit(solution)/shard_map/ppermute | solution.py:20
  16.5 6.2 %collective-permute-done = f32[1,256,512]{2,1,0:T(8,128)S(1)} collective-permute-done((f32[1,256,512]{2,1,0:T(8,128)S(1)}, f32[1,256,512]{2,1,0:T(8,128)S(1)}, u32[]{:S(2)}, u32[]{:S(2)}) %collective-permute-start) | collective-permute-done | bytes 524320 | tf_op jit(solution)/shard_map/ppermute | solution.py:18
  22.7 2.4 collective-permute-done.1
  25.1 9.8 %multiply_add_fusion.3 = f32[8,256,512]{2,1,0:T(8,128)S(1)} fusion(f32[8,256,512]{2,1,0:T(8,128)} %param.3, f32[1,256,512]{2,1,0:T(8,128)S(1)} %collective-permute-done.1, f32[1,256,512]{2,1,0:T(8,128)S(1)} %collective-permute-done), kind=kLoop, calls=%fused_computation.19 | loop fusion | flops 28311552 | bytes 9437184 | tf_op jit(solution)/shard_map/add | solution.py:36
  35.1 3.7 collective-permute-start.2
  38.8 4.4 collective-permute-start.3
  43.2 7.8 %collective-permute-done.2 = f32[1,256,512]{2,1,0:T(8,128)S(1)} collective-permute-done((f32[1,256,512]{2,1,0:T(8,128)S(1)}, f32[1,256,512]{2,1,0:T(8,128)S(1)}, u32[]{:S(2)}, u32[]{:S(2)}) %collective-permute-start.2) | collective-permute-done | bytes 524320 | tf_op jit(solution)/shard_map/ppermute | solution.py:18
  51.0 4.5 multiply_add_fusion.2
  55.5 2.0 copy-done.1
  57.6 4.6 collective-permute-start.4
  62.2 3.3 collective-permute-start.5
  65.7 6.6 %collective-permute-done.4 = f32[1,256,512]{2,1,0:T(8,128)S(1)} collective-permute-done((f32[1,256,512]{2,1,0:T(8,128)S(1)}, f32[1,256,512]{2,1,0:T(8,128)S(1)}, u32[]{:S(2)}, u32[]{:S(2)}) %collective-permute-start.4) | collective-permute-done | bytes 524320 | tf_op jit(solution)/shard_map/ppermute | solution.py:18
  72.3 1.6 collective-permute-done.5
  73.9 10.0 %multiply_add_fusion.1 = f32[8,256,512]{2,1,0:T(8,128)S(1)} fusion(f32[8,256,512]{2,1,0:T(8,128)} %copy-done.1, f32[1,256,512]{2,1,0:T(8,128)S(1)} %collective-permute-done.5, f32[1,256,512]{2,1,0:T(8,128)S(1)} %collective-permute-done.4), kind=kLoop, calls=%fused_computation.17 | loop fusion | flops 28311552 | bytes 9437184 | tf_op jit(solution)/shard_map/add | solution.py:36
  83.9 4.1 collective-permute-start.6
  88.1 4.0 collective-permute-start.7
  92.1 15.5 %collective-permute-done.6 = f32[1,256,512]{2,1,0:T(8,128)S(1)} collective-permute-done((f32[1,256,512]{2,1,0:T(8,128)S(1)}, f32[1,256,512]{2,1,0:T(8,128)S(1)}, u32[]{:S(2)}, u32[]{:S(2)}) %collective-permute-start.6) | collective-permute-done | bytes 524320 | tf_op jit(solution)/shard_map/ppermute | solution.py:18
  107.6 5.5 %multiply_add_fusion = f32[8,256,512]{2,1,0:T(8,128)} fusion(f32[8,256,512]{2,1,0:T(8,128)S(1)} %multiply_add_fusion.1, f32[1,256,512]{2,1,0:T(8,128)S(1)} %collective-permute-done.7, f32[1,256,512]{2,1,0:T(8,128)S(1)} %collective-permute-done.6), kind=kLoop, calls=%fused_computation.16 | loop fusion | flops 28311552 | bytes 9437184 | tf_op jit(solution)/shard_map/add | solution.py:36
  113.1 25.4 %all-gather.4.cloned.1.call-done = f32[256,2048]{1,0:T(8,128)} async-done(((f32[16,2048]{1,0:T(8,128)}), f32[256,2048]{1,0:T(8,128)}) %all-gather.4.cloned.1.call-update) | async-done | bytes 2097168 | tf_op jit(solution)/shard_map/all_gather | solution.py:62
  138.5 4.9 fusion.17
  143.7 8.6 %convolution_bitcast_fusion = f32[256,512]{0,1:T(8,128)S(1)} fusion(f32[2048,512]{1,0:T(8,128)} %bitcast.15, f32[256,2048]{1,0:T(8,128)S(1)} %copy-done), kind=kOutput, calls=%fused_computation.20 | convolution fusion | flops 3221225472 | bytes 6815744 | tf_op jit(solution)/shard_map/dot_general | solution.py:40
  153.4 24.2 %all_gather.16 = f32[256,512]{1,0:T(8,128)S(1)} all-gather(f32[16,512]{1,0:T(8,128)S(1)} %copy-done.3), channel_id=1, replica_groups=mesh['pix'=16,'tm'=16] {'pix'}, dimensions={0}, use_global_device_ids=true | all-gather | bytes 557056 | tf_op jit(solution)/shard_map/all_gather | solution.py:63
  177.5 99.7 %all-reduce.6.cloned.1.call-done = f32[256,256]{1,0:T(8,128)} async-done(((f32[256,256]{1,0:T(8,128)}), f32[256,256]{1,0:T(8,128)}) %all-reduce.6.cloned.1.call-update) | async-done | bytes 262160 | tf_op jit(solution)/shard_map/psum | solution.py:68
  277.2 85.2 %reduce-scatter.7.cloned.1.call-done = f32[16,512]{1,0:T(8,128)} async-done(((f32[256,512]{1,0:T(8,128)}), f32[16,512]{1,0:T(8,128)}) %reduce-scatter.7.cloned.1.call-update) | async-done | bytes 32784 | tf_op jit(solution)/shard_map/reduce_scatter | solution.py:67
  363.5 21.5 %all_gather.17 = f32[256,512]{1,0:T(8,128)S(1)} all-gather(f32[16,512]{1,0:T(8,128)S(1)} %convolution_divide_fusion), channel_id=1, replica_groups=mesh['pix'=16,'tm'=16] {'pix'}, dimensions={0}, use_global_device_ids=true | all-gather | bytes 557056 | tf_op jit(solution)/shard_map/all_gather | solution.py:71
  385.0 1.3 fusion.19
  386.4 7.2 %fusion.18 = f32[256,2048]{1,0:T(8,128)} fusion(f32[256,512]{1,0:T(8,128)S(1)} %all_gather.17, f32[2048,512]{1,0:T(8,128)} %bitcast.16), kind=kOutput, calls=%fused_computation.33 | convolution fusion | flops 3221225472 | bytes 6815744 | tf_op jit(solution)/shard_map/dot_general | solution.py:44
  393.7 69.6 %all-gather.6.cloned.1.call-done = f32[4096,256]{1,0:T(8,128)} async-done(((f32[256,256]{1,0:T(8,128)}), f32[4096,256]{1,0:T(8,128)}) %all-gather.6.cloned.1.call-update) | async-done | bytes 4194320 | tf_op jit(solution)/shard_map/all_gather | solution.py:78
  463.2 2.5 reduce_sum.9
  466.8 70.6 %reduce-scatter.5.cloned.1.call-done = f32[16,2048]{1,0:T(8,128)} async-done(((f32[256,2048]{1,0:T(8,128)}), f32[16,2048]{1,0:T(8,128)}) %reduce-scatter.5.cloned.1.call-update) | async-done | bytes 131088 | tf_op jit(solution)/shard_map/reduce_scatter | solution.py:75
  537.4 1.6 multiply_divide_fusion
  (28 shorter events, 5.2 us)
Async XLA Ops:
  7.2 131.3 %all-gather.4.cloned.1.call-start = ((), (), s32[]{:S(2)}) async-start(), calls=%async_computation.2 | async-start | bytes 2228224 | tf_op jit(solution)/shard_map/all_gather | solution.py:62
  8.5 14.2 %collective-permute-start = (f32[1,256,512]{2,1,0:T(8,128)S(1)}, f32[1,256,512]{2,1,0:T(8,128)S(1)}, u32[]{:S(2)}, u32[]{:S(2)}) collective-permute-start(f32[1,256,512]{2,1,0:T(8,128)S(1)} %get-tuple-element.12), channel_id=1, source_target_pairs={{0,16},{16,32},{32,48},{48,64},{64,80},{80,96},{96,112},{112,128},... | collective-permute-start | bytes 1572872 | tf_op jit(solution)/shard_map/ppermute | solution.py:18
  10.4 14.7 %collective-permute-start.1 = (f32[1,256,512]{2,1,0:T(8,128)S(1)}, f32[1,256,512]{2,1,0:T(8,128)S(1)}, u32[]{:S(2)}, u32[]{:S(2)}) collective-permute-start(f32[1,256,512]{2,1,0:T(8,128)S(1)} %get-tuple-element.13), channel_id=1, source_target_pairs={{16,0},{32,16},{48,32},{64,48},{80,64},{96,80},{112,96},{128,112},... | collective-permute-start | bytes 1572872 | tf_op jit(solution)/shard_map/ppermute | solution.py:20
  35.1 15.9 %collective-permute-start.2 = (f32[1,256,512]{2,1,0:T(8,128)S(1)}, f32[1,256,512]{2,1,0:T(8,128)S(1)}, u32[]{:S(2)}, u32[]{:S(2)}) collective-permute-start(f32[1,256,512]{2,1,0:T(8,128)S(1)} %get-tuple-element.10), channel_id=1, source_target_pairs={{0,16},{16,32},{32,48},{48,64},{64,80},{80,96},{96,112},{112,128},... | collective-permute-start | bytes 1572872 | tf_op jit(solution)/shard_map/ppermute | solution.py:18
  38.8 12.2 %collective-permute-start.3 = (f32[1,256,512]{2,1,0:T(8,128)S(1)}, f32[1,256,512]{2,1,0:T(8,128)S(1)}, u32[]{:S(2)}, u32[]{:S(2)}) collective-permute-start(f32[1,256,512]{2,1,0:T(8,128)S(1)} %get-tuple-element.11), channel_id=1, source_target_pairs={{16,0},{32,16},{48,32},{64,48},{80,64},{96,80},{112,96},{128,112},... | collective-permute-start | bytes 1572872 | tf_op jit(solution)/shard_map/ppermute | solution.py:20
  55.5 2.0 copy-start.1
  57.6 14.6 %collective-permute-start.4 = (f32[1,256,512]{2,1,0:T(8,128)S(1)}, f32[1,256,512]{2,1,0:T(8,128)S(1)}, u32[]{:S(2)}, u32[]{:S(2)}) collective-permute-start(f32[1,256,512]{2,1,0:T(8,128)S(1)} %get-tuple-element.8), channel_id=1, source_target_pairs={{0,16},{16,32},{32,48},{48,64},{64,80},{80,96},{96,112},{112,128},... | collective-permute-start | bytes 1572872 | tf_op jit(solution)/shard_map/ppermute | solution.py:18
  62.2 11.6 %collective-permute-start.5 = (f32[1,256,512]{2,1,0:T(8,128)S(1)}, f32[1,256,512]{2,1,0:T(8,128)S(1)}, u32[]{:S(2)}, u32[]{:S(2)}) collective-permute-start(f32[1,256,512]{2,1,0:T(8,128)S(1)} %get-tuple-element.9), channel_id=1, source_target_pairs={{16,0},{32,16},{48,32},{64,48},{80,64},{96,80},{112,96},{128,112},... | collective-permute-start | bytes 1572872 | tf_op jit(solution)/shard_map/ppermute | solution.py:20
  65.6 211.6 %all-reduce.6.cloned.1.call-start = ((), (), s32[]{:S(2)}) async-start(), calls=%async_computation.3 | async-start | bytes 524288 | tf_op jit(solution)/shard_map/psum | solution.py:68
  83.9 23.6 %collective-permute-start.6 = (f32[1,256,512]{2,1,0:T(8,128)S(1)}, f32[1,256,512]{2,1,0:T(8,128)S(1)}, u32[]{:S(2)}, u32[]{:S(2)}) collective-permute-start(f32[1,256,512]{2,1,0:T(8,128)S(1)} %get-tuple-element.6), channel_id=1, source_target_pairs={{0,16},{16,32},{32,48},{48,64},{64,80},{80,96},{96,112},{112,128},... | collective-permute-start | bytes 1572872 | tf_op jit(solution)/shard_map/ppermute | solution.py:18
  88.1 19.5 %collective-permute-start.7 = (f32[1,256,512]{2,1,0:T(8,128)S(1)}, f32[1,256,512]{2,1,0:T(8,128)S(1)}, u32[]{:S(2)}, u32[]{:S(2)}) collective-permute-start(f32[1,256,512]{2,1,0:T(8,128)S(1)} %get-tuple-element.7), channel_id=1, source_target_pairs={{16,0},{32,16},{48,32},{64,48},{80,64},{96,80},{112,96},{128,112},... | collective-permute-start | bytes 1572872 | tf_op jit(solution)/shard_map/ppermute | solution.py:20
  138.5 5.2 copy-start
  143.5 218.9 %reduce-scatter.7.cloned.1.call-start = ((), (), s32[]{:S(2)}) async-start(), calls=%async_computation.6 | async-start | bytes 557056 | tf_op jit(solution)/shard_map/reduce_scatter | solution.py:67
  143.7 9.7 %copy-start.3 = (f32[16,512]{1,0:T(8,128)S(1)}, f32[16,512]{1,0:T(8,128)}, u32[]{:S(2)}) copy-start(f32[16,512]{1,0:T(8,128)} %param.5) | copy-start | bytes 98308
  153.3 309.9 %all-gather.6.cloned.1.call-start = ((), (), s32[]{:S(2)}) async-start(), calls=%async_computation.5 | async-start | bytes 4456448 | tf_op jit(solution)/shard_map/all_gather | solution.py:78
  363.5 30.1 %copy-start.4 = (f32[16,512]{1,0:T(8,128)}, f32[16,512]{1,0:T(8,128)S(1)}, u32[]{:S(2)}) copy-start(f32[16,512]{1,0:T(8,128)S(1)} %convolution_divide_fusion) | copy-start | bytes 98308
  386.4 151.0 %reduce-scatter.5.cloned.1.call-start = ((), (), s32[]{:S(2)}) async-start(), calls=%async_computation.4 | async-start | bytes 2228224 | tf_op jit(solution)/shard_map/reduce_scatter | solution.py:75
  393.6 143.7 %copy-start.2 = (f32[16,2048]{1,0:T(8,128)S(1)}, f32[16,2048]{1,0:T(8,128)}, u32[]{:S(2)}) copy-start(f32[16,2048]{1,0:T(8,128)} %param.4) | copy-start | bytes 393220
Sparse Core Ops, SparseCore 0:
  65.7 72.7 all-gather.3
  143.6 133.5 all-reduce.5
  281.7 80.6 reduce-scatter.6
  386.5 76.6 all-gather.5
  465.6 71.7 reduce-scatter.4
